TPU v7x, 512 devices: a whole 4x8x8 slice. The times are simulated.
512 devices in a mesh: op: 16 (over y, core), lsec: 8 (over z), rsec: 4 (over x).
Axes of the slice: x: 4, y: 8, z: 8, core: 2. Of those that a mesh axis runs over, the one named last changes fastest.
Arguments:
- wavefn: float32 [32, 16, 128, 128], P('lsec', 'rsec'), may hold values from -6 to 6
- left_ops: float32 [112, 32, 128, 128], P('op', 'lsec'), may hold values from -0.5 to 0.5
- right_ops: float32 [112, 16, 128, 128], P('op', 'rsec'), may hold values from -0.046875 to 0.046875
- term_shift: int32 [112], P('op'), may hold values from 0 to 1
Outputs:
- sigma: float32 [32, 16, 128, 128], P('lsec', 'rsec', 'op')
All inputs are finite; a program needn't handle non-finite values.
Results may differ from a plain program's by a relative error of at most 0.0001.
Values sent between devices are 32-bit elements; how exact they have to be, the bound alone decides.
A program may use at most 64 MiB of HBM per device.

v0:
```python
import jax
import jax.numpy as jnp
from jax import lax
from jax.sharding import PartitionSpec as P


def from_behind(value, axis, by):
    count = lax.axis_size(axis)
    return lax.ppermute(value, axis, [(i, (i + by) % count) for i in range(count)])


def roll_slots(block, carry, dim):
    count = block.shape[dim]
    widths = [(0, 0)] * block.ndim
    widths[dim] = (1, 1)
    padded = jnp.pad(block, widths)
    return lax.dynamic_slice_in_dim(padded, 1 - carry, count, dim)


def left_move(block, steps):
    count = lax.axis_size("lsec")
    mine = lax.axis_index("lsec")
    moved = from_behind(block, "lsec", steps)
    source = (mine - steps) % count
    carry = (source + steps - mine) // count
    return roll_slots(moved, carry, 0)


def right_move(block, steps):
    count = lax.axis_size("rsec")
    mine = lax.axis_index("rsec")
    moved = from_behind(block, "rsec", steps)
    source = (mine - steps) % count
    carry = (source + steps - mine) // count
    return roll_slots(moved, carry, 1)


def shards(wavefn, left_ops, right_ops, term_shift):
    high = lax.Precision.HIGHEST
    inner = jnp.einsum("tlij,lrjk->tlrik", left_ops, wavefn, precision=high)
    weight = term_shift.astype(jnp.float32)[:, None, None, None, None]
    rising = jnp.einsum("tlrik,trmk->lrim", inner * weight, right_ops, precision=high)
    falling = jnp.einsum("tlrik,trmk->lrim", inner * (1.0 - weight), right_ops, precision=high)
    moved = right_move(left_move(rising, 1), -1) + right_move(left_move(falling, -1), 1)
    return lax.psum_scatter(moved, "op", scatter_dimension=2, tiled=True)


def solution(mesh):
    placed = (
        P("lsec", "rsec", None, None),
        P("op", "lsec", None, None),
        P("op", "rsec", None, None),
        P("op"),
    )
    return jax.shard_map(
        shards, mesh=mesh, in_specs=placed, out_specs=P("lsec", "rsec", "op", None), check_vma=False
    )
```

profile of v0, /device:TPU:1, one launch (start us, length us, event | category | flops | bytes accessed | tf_op | source)
XLA Modules:
  0.0 177.3 jit_solution(8773390799693386523)
XLA Ops:
  6.5 0.0 copy-start
  6.5 0.0 reduce-scatter.2.cloned.1.call-start
  6.5 0.8 broadcast_subtract_fusion
  7.3 0.7 convert_element_type.9
  8.0 0.1 copy-done
  8.1 0.0 copy-start.1
  8.1 9.8 %multiply_bitcast_fusion = (f32[7,4,4,128,128]{3,4,0,2,1:T(8,128)S(1)}, f32[7,4,4,128,128]{3,4,0,2,1:T(8,128)S(1)}) fusion(f32[7]{0:T(128)S(1)} %broadcast_subtract_fusion, f32[7]{0:T(128)S(1)} %convert_element_type.9, f32[4,4,128,128]{3,2,1,0:T(8,128)} %param.4, f32[7,4,128,128]{3,2,1,0:T(8,128)S(1)} %copy-done), kind=kOutput, calls=%fused_computation.4 | convolution fusion | flops 2822242304 | bytes 17563704 | tf_op jit(solution)/shard_map/tlij,lrjk->tlrik/dot_general | solution.py:40
  17.9 0.0 copy-done.1
  17.9 13.3 %fusion.13 = f32[4,4,128,128]{3,2,0,1:T(8,128)} fusion(f32[7,4,4,128,128]{3,4,0,2,1:T(8,128)S(1)} %get-tuple-element.5, f32[7,4,128,128]{3,2,1,0:T(8,128)S(1)} %copy-done.1), kind=kOutput, calls=%fused_computation.15 | convolution fusion | flops 2818572288 | bytes 10223616 | tf_op jit(solution)/shard_map/tlrik,trmk->lrim/dot_general | solution.py:43
  31.2 11.7 %collective-permute-start.2 = (f32[4,4,128,128]{3,2,0,1:T(8,128)}, f32[4,4,128,128]{3,2,0,1:T(8,128)}, u32[]{:S(2)}, u32[]{:S(2)}) collective-permute-start(f32[4,4,128,128]{3,2,0,1:T(8,128)} %fusion.13), channel_id=1, source_target_pairs={{0,28},{4,0},{8,4},{12,8},{16,12},{20,16},{24,20},{28,24},{1,29},{... | collective-permute-start | bytes 3145736 | tf_op jit(solution)/shard_map/ppermute | solution.py:9
  42.9 12.0 %fusion.8 = f32[4,4,128,128]{3,2,0,1:T(8,128)S(1)} fusion(f32[7,4,4,128,128]{3,4,0,2,1:T(8,128)S(1)} %get-tuple-element.6, f32[7,4,128,128]{3,2,1,0:T(8,128)S(1)} %copy-done.1), kind=kOutput, calls=%fused_computation.14 | convolution fusion | flops 2818572288 | bytes 10223616 | tf_op jit(solution)/shard_map/tlrik,trmk->lrim/dot_general | solution.py:42
  54.9 1.9 %collective-permute-start = (f32[4,4,128,128]{3,2,0,1:T(8,128)S(1)}, f32[4,4,128,128]{3,2,0,1:T(8,128)}, u32[]{:S(2)}, u32[]{:S(2)}) collective-permute-start(f32[4,4,128,128]{3,2,0,1:T(8,128)S(1)} %fusion.8), channel_id=1, source_target_pairs={{0,4},{4,8},{8,12},{12,16},{16,20},{20,24},{24,28},{28,0},{1,5},{5... | collective-permute-start | bytes 3145736 | tf_op jit(solution)/shard_map/ppermute | solution.py:9
  56.9 7.9 %collective-permute-done.2 = f32[4,4,128,128]{3,2,0,1:T(8,128)} collective-permute-done((f32[4,4,128,128]{3,2,0,1:T(8,128)}, f32[4,4,128,128]{3,2,0,1:T(8,128)}, u32[]{:S(2)}, u32[]{:S(2)}) %collective-permute-start.2) | collective-permute-done | bytes 1048608 | tf_op jit(solution)/shard_map/ppermute | solution.py:9
  64.8 2.3 %pad_dynamic-slice_fusion.1 = f32[4,4,128,128]{3,2,0,1:T(8,128)} fusion(s32[]{:T(128)S(6)} %select_n.52, f32[4,4,128,128]{3,2,0,1:T(8,128)} %collective-permute-done.2), kind=kLoop, calls=%fused_computation.11 | loop fusion | bytes 2097156 | tf_op jit(solution)/shard_map/dynamic_slice | solution.py:17
  67.1 3.1 %collective-permute-start.3 = (f32[4,4,128,128]{3,2,0,1:T(8,128)}, f32[4,4,128,128]{3,2,0,1:T(8,128)}, u32[]{:S(2)}, u32[]{:S(2)}) collective-permute-start(f32[4,4,128,128]{3,2,0,1:T(8,128)} %pad_dynamic-slice_fusion.1), channel_id=1, source_target_pairs={{0,1},{1,2},{2,3},{3,0},{4,5},{5,6},{6,7},{7,4},{8,9},{9,10},{10,1... | collective-permute-start | bytes 3145736 | tf_op jit(solution)/shard_map/ppermute | solution.py:9
  70.2 11.6 %collective-permute-done = f32[4,4,128,128]{3,2,0,1:T(8,128)} collective-permute-done((f32[4,4,128,128]{3,2,0,1:T(8,128)S(1)}, f32[4,4,128,128]{3,2,0,1:T(8,128)}, u32[]{:S(2)}, u32[]{:S(2)}) %collective-permute-start) | collective-permute-done | bytes 1048608 | tf_op jit(solution)/shard_map/ppermute | solution.py:9
  81.9 1.2 pad_dynamic-slice_fusion.3
  83.1 4.4 %collective-permute-start.1 = (f32[4,4,128,128]{3,2,0,1:T(8,128)S(1)}, f32[4,4,128,128]{3,2,0,1:T(8,128)}, u32[]{:S(2)}, u32[]{:S(2)}) collective-permute-start(f32[4,4,128,128]{3,2,0,1:T(8,128)S(1)} %pad_dynamic-slice_fusion.3), channel_id=1, source_target_pairs={{0,3},{1,0},{2,1},{3,2},{4,7},{5,4},{6,5},{7,6},{8,11},{9,8},{10,9... | collective-permute-start | bytes 3145736 | tf_op jit(solution)/shard_map/ppermute | solution.py:9
  87.5 6.2 %collective-permute-done.3 = f32[4,4,128,128]{3,2,0,1:T(8,128)} collective-permute-done((f32[4,4,128,128]{3,2,0,1:T(8,128)}, f32[4,4,128,128]{3,2,0,1:T(8,128)}, u32[]{:S(2)}, u32[]{:S(2)}) %collective-permute-start.3) | collective-permute-done | bytes 1048608 | tf_op jit(solution)/shard_map/ppermute | solution.py:9
  93.7 14.5 %collective-permute-done.1 = f32[4,4,128,128]{3,2,0,1:T(8,128)} collective-permute-done((f32[4,4,128,128]{3,2,0,1:T(8,128)S(1)}, f32[4,4,128,128]{3,2,0,1:T(8,128)}, u32[]{:S(2)}, u32[]{:S(2)}) %collective-permute-start.1) | collective-permute-done | bytes 1048608 | tf_op jit(solution)/shard_map/ppermute | solution.py:9
  108.2 2.6 %fusion.18 = f32[4,4,128,128]{3,2,0,1:T(8,128)} fusion(s32[]{:T(128)S(6)} %select_n.49, f32[4,4,128,128]{3,2,0,1:T(8,128)} %collective-permute-done.1, s32[]{:T(128)S(6)} %select_n.55, f32[4,4,128,128]{3,2,0,1:T(8,128)} %collective-permute-done.3), kind=kLoop, calls=%fused_computation.16 | loop fusion | flops 262144 | bytes 3145736 | tf_op jit(solution)/shard_map/add | solution.py:44
  110.7 0.0 reduce-scatter.2.cloned.1.call-update
  110.8 58.2 %reduce-scatter.2.cloned.1.call-done = f32[4,4,8,128]{3,2,0,1:T(8,128)} async-done(((f32[4,4,128,128]{3,2,0,1:T(8,128)}), f32[4,4,8,128]{3,2,0,1:T(8,128)}) %reduce-scatter.2.cloned.1.call-update) | async-done | bytes 65552 | tf_op jit(solution)/shard_map/reduce_scatter | solution.py:45
  168.9 1.5 copy.11
Async XLA Ops:
  6.5 1.5 copy-start
  6.5 162.4 %reduce-scatter.2.cloned.1.call-start = ((), (), s32[]{:S(2)}) async-start(), calls=%async_computation.1 | async-start | bytes 1114112 | tf_op jit(solution)/shard_map/reduce_scatter | solution.py:45
  8.1 9.8 %copy-start.1 = (f32[7,4,128,128]{3,2,1,0:T(8,128)S(1)}, f32[7,4,128,128]{3,2,1,0:T(8,128)}, u32[]{:S(2)}) copy-start(f32[7,4,128,128]{3,2,1,0:T(8,128)} %param.6) | copy-start | bytes 5505028
  31.2 33.6 %collective-permute-start.2 = (f32[4,4,128,128]{3,2,0,1:T(8,128)}, f32[4,4,128,128]{3,2,0,1:T(8,128)}, u32[]{:S(2)}, u32[]{:S(2)}) collective-permute-start(f32[4,4,128,128]{3,2,0,1:T(8,128)} %fusion.13), channel_id=1, source_target_pairs={{0,28},{4,0},{8,4},{12,8},{16,12},{20,16},{24,20},{28,24},{1,29},{... | collective-permute-start | bytes 3145736 | tf_op jit(solution)/shard_map/ppermute | solution.py:9
  54.9 27.0 %collective-permute-start = (f32[4,4,128,128]{3,2,0,1:T(8,128)S(1)}, f32[4,4,128,128]{3,2,0,1:T(8,128)}, u32[]{:S(2)}, u32[]{:S(2)}) collective-permute-start(f32[4,4,128,128]{3,2,0,1:T(8,128)S(1)} %fusion.8), channel_id=1, source_target_pairs={{0,4},{4,8},{8,12},{12,16},{16,20},{20,24},{24,28},{28,0},{1,5},{5... | collective-permute-start | bytes 3145736 | tf_op jit(solution)/shard_map/ppermute | solution.py:9
  67.1 26.6 %collective-permute-start.3 = (f32[4,4,128,128]{3,2,0,1:T(8,128)}, f32[4,4,128,128]{3,2,0,1:T(8,128)}, u32[]{:S(2)}, u32[]{:S(2)}) collective-permute-start(f32[4,4,128,128]{3,2,0,1:T(8,128)} %pad_dynamic-slice_fusion.1), channel_id=1, source_target_pairs={{0,1},{1,2},{2,3},{3,0},{4,5},{5,6},{6,7},{7,4},{8,9},{9,10},{10,1... | collective-permute-start | bytes 3145736 | tf_op jit(solution)/shard_map/ppermute | solution.py:9
  83.1 25.1 %collective-permute-start.1 = (f32[4,4,128,128]{3,2,0,1:T(8,128)S(1)}, f32[4,4,128,128]{3,2,0,1:T(8,128)}, u32[]{:S(2)}, u32[]{:S(2)}) collective-permute-start(f32[4,4,128,128]{3,2,0,1:T(8,128)S(1)} %pad_dynamic-slice_fusion.3), channel_id=1, source_target_pairs={{0,3},{1,0},{2,1},{3,2},{4,7},{5,4},{6,5},{7,6},{8,11},{9,8},{10,9... | collective-permute-start | bytes 3145736 | tf_op jit(solution)/shard_map/ppermute | solution.py:9
Sparse Core Ops, SparseCore 0:
  110.9 58.0 reduce-scatter.1
where the time goes:
time: 179 us; the launch traced here: 177 us
  waiting for transfers between devices  98.3 us (55%)
  matrix products  35.1 us (20%)
  starting transfers between devices  21.1 us (12%)
  between operations  13.6 us (8%)
  local copies, waits for them, and re-layouts  5.08 us (3%)
  other arithmetic  4.04 us (2%)
    reduce_scatter x1, waiting for transfers between devices, shards(): return lax.psum_scatter(moved, 'op', scatter_dimension=2, tiled=True)  58.2 us
    ppermute x4, waiting for transfers between devices, from_behind(): lax.ppermute(value, axis, [(i, (i + by) % count) for i in range(count)])  40.1 us
    ppermute x4, starting transfers between devices, from_behind(): lax.ppermute(value, axis, [(i, (i + by) % count) for i in range(count)])  21.1 us
    dot_general x1, matrix products, shards(): jnp.einsum('tlrik,trmk->lrim', inner * (1.0 - weight), right_ops, precisi...  13.3 us
    dot_general x1, matrix products, shards(): jnp.einsum('tlrik,trmk->lrim', inner * weight, right_ops, precision=high)  12 us
    dot_general x1, matrix products, shards(): inner = jnp.einsum('tlij,lrjk->tlrik', left_ops, wavefn, precision=high)  9.81 us
  transfers between devices with their start and end apart: 5, of which 5 were waited for; matrix products, arithmetic and copies ran while one was open for 9% of the time, Pallas kernels for 0%

commit v1 on v0

v1 whole, which is shorter than its diff:
```python
import jax
import jax.numpy as jnp
from jax import lax
from jax.experimental import pallas as pl
from jax.experimental.pallas import tpu as pltpu
from jax.sharding import PartitionSpec as P

MESH = pl.DeviceIdType.MESH
F32 = jnp.float32
BF16 = jnp.bfloat16


def split(value):
    high = value.astype(BF16)
    return high, (value - high.astype(F32)).astype(BF16)


def kernel(shift, psi, lop, rop, out, lcat, pcat, wcat, wlow, x, acc, peer, ring, moved, send, recv):
    terms, nl = lop.shape[0], lop.shape[1]
    nr = psi.shape[1]
    s = psi.shape[2]
    ny = lop.shape[2]
    half = s // 2
    depth = terms * s

    op = lax.axis_index("op")
    lsec = lax.axis_index("lsec")
    rsec = lax.axis_index("rsec")
    n_lsec, n_rsec = lax.axis_size("lsec"), lax.axis_size("rsec")
    y, core = op // 2, op % 2
    partner = {"op": y * 2 + (1 - core)}
    ahead = {"op": ((y + 1) % ny) * 2 + core}
    behind = {"op": ((y + ny - 1) % ny) * 2 + core}
    raise_to = {"lsec": (lsec + 1) % n_lsec, "rsec": (rsec + n_rsec - 1) % n_rsec}
    lower_to = {"lsec": (lsec + n_lsec - 1) % n_lsec, "rsec": (rsec + 1) % n_rsec}

    barrier = pltpu.get_barrier_semaphore()
    for who in (partner, ahead, behind, raise_to, lower_to):
        pl.semaphore_signal(barrier, inc=1, device_id=who, device_id_type=MESH)

    for l in range(nl):
        for t in range(terms):
            for h in range(2):
                c = (1 - core) if h == 0 else core
                high, low = split(lop[t, l, :, c].reshape(half, s))
                rows = pl.ds((t * 2 + h) * half, half)
                lcat[l, rows, 0:s] = high
                lcat[l, rows, s : 2 * s] = low

    for r in range(nr):
        for t in range(terms):
            weight = shift[t].astype(F32)
            for k, w in enumerate((weight, 1.0 - weight)):
                high, low = split(rop[t, r] * w)
                rows = pl.ds(k * s, s)
                wcat[r, rows, t * s : (t + 1) * s] = high
                wcat[r, rows, depth + t * s : depth + (t + 1) * s] = high
                wlow[r, rows, t * s : (t + 1) * s] = low

    def remote(src, dst, n, r, who):
        return pltpu.make_async_remote_copy(
            src_ref=src, dst_ref=dst, send_sem=send.at[r, n], recv_sem=recv.at[r, n], device_id=who, device_id_type=MESH
        )

    def chunk(r, far, k=None):
        at = acc.at[r, 1, :, (y + far + ny) % ny]
        return at if k is None else at.at[:, :, pl.ds(k * s, s)]

    pending = []

    def exchange(r):
        return remote(acc.at[r, 0], peer.at[r], 0, r, partner)

    def ring_copy(r, d, step):
        far = (4 - step) if d == 0 else (step - 4)
        who = ahead if d == 0 else behind
        n = 1 + d * 4 + step
        if step == 0:
            return remote(chunk(r, far, d), ring.at[r, d, step, :, :, pl.ds(d * s, s)], n, r, who)
        return remote(chunk(r, far), ring.at[r, d, step], n, r, who)

    def move_copy(r, k):
        who = raise_to if k == 0 else lower_to
        return remote(chunk(r, 0, k), moved.at[k, :, r], 9 + k, r, who)

    def multiply(r):
        for l in range(nl):
            high, low = split(psi[l, r])
            for k in range(2):
                pcat[l, k * s : (k + 1) * s, 0:s] = high
                pcat[l, k * s : (k + 1) * s, s : 2 * s] = low
        for l in range(nl):
            both = jnp.dot(lcat[l], pcat[l], preferred_element_type=F32)
            high, low = split(both[:, 0:s] + both[:, s : 2 * s])
            for t in range(terms):
                for h in range(2):
                    rows = slice((t * 2 + h) * half, (t * 2 + h + 1) * half)
                    at = pl.ds(h * nl * half + l * half, half)
                    x[at, t * s : (t + 1) * s] = high[rows]
                    x[at, depth + t * s : depth + (t + 1) * s] = low[rows]
        nt = (((1,), (1,)), ((), ()))
        total = lax.dot_general(x[...], wcat[r], nt, preferred_element_type=F32)
        total += lax.dot_general(x[:, 0:depth], wlow[r], nt, preferred_element_type=F32)
        acc[r] = total.reshape(2, nl, ny, 8, 2 * s)

    for r in range(nr):
        multiply(r)
    pl.semaphore_wait(barrier, 5)
    for r in range(nr):
        exchange(r).start()
    for r in range(nr):
        exchange(r).wait_recv()
        acc[r, 1] += peer[r]
        for d in range(2):
            ring_copy(r, d, 0).start()
    for step in range(4):
        for r in range(nr):
            for d in range(2):
                ring_copy(r, d, step).wait_recv()
                far = (3 - step) if d == 0 else (step - 3)
                at = (y + far + ny) % ny
                if step == 0:
                    lanes = pl.ds(d * s, s)
                    acc[r, 1, :, at, :, lanes] += ring[r, d, step, :, :, lanes]
                else:
                    acc[r, 1, :, at] += ring[r, d, step]
                if step < 3:
                    ring_copy(r, d, step + 1).start()
            if step == 3:
                for k in range(2):
                    move_copy(r, k).start()
    for r in range(nr):
        for k in range(2):
            move_copy(r, k).wait_recv()

    up_l = (lsec == 0).astype(jnp.int32)
    up_r = (rsec == n_rsec - 1).astype(jnp.int32)
    down_l = (lsec == n_lsec - 1).astype(jnp.int32)
    down_r = (rsec == 0).astype(jnp.int32)

    def picked(k, l, r):
        inside = (l >= 0) & (l < nl) & (r >= 0) & (r < nr)
        tile = moved[k, jnp.clip(l, 0, nl - 1), jnp.clip(r, 0, nr - 1)]
        return jnp.where(inside, tile, 0.0)

    for l in range(nl):
        for r in range(nr):
            out[l, r] = picked(0, l - up_l, r + up_r) + picked(1, l + down_l, r - down_r)

    for r in range(nr):
        exchange(r).wait_send()
        for d in range(2):
            for step in range(4):
                ring_copy(r, d, step).wait_send()
        for k in range(2):
            move_copy(r, k).wait_send()


def shards(wavefn, left_ops, right_ops, term_shift):
    nl, nr, s = wavefn.shape[:3]
    terms = left_ops.shape[0]
    ny = lax.axis_size("op") // 2
    vmem = pl.BlockSpec(memory_space=pltpu.VMEM)
    return pl.pallas_call(
        kernel,
        out_shape=jax.ShapeDtypeStruct((nl, nr, s // (2 * ny), s), F32),
        in_specs=[pl.BlockSpec(memory_space=pltpu.SMEM), vmem, vmem, vmem],
        out_specs=vmem,
        scratch_shapes=[
            pltpu.VMEM((nl, terms * s, 2 * s), BF16),
            pltpu.VMEM((nl, 2 * s, 2 * s), BF16),
            pltpu.VMEM((nr, 2 * s, 2 * terms * s), BF16),
            pltpu.VMEM((nr, 2 * s, terms * s), BF16),
            pltpu.VMEM((nl * s, 2 * terms * s), BF16),
            pltpu.VMEM((nr, 2, nl, ny, 8, 2 * s), F32),
            pltpu.VMEM((nr, nl, ny, 8, 2 * s), F32),
            pltpu.VMEM((nr, 2, 4, nl, 8, 2 * s), F32),
            pltpu.VMEM((2, nl, nr, 8, s), F32),
            pltpu.SemaphoreType.DMA((nr, 11)),
            pltpu.SemaphoreType.DMA((nr, 11)),
        ],
        compiler_params=pltpu.CompilerParams(collective_id=0, has_side_effects=True, vmem_limit_bytes=60 * 2**20),
        name="sigma",
    )(term_shift, wavefn, left_ops.reshape(terms, nl, ny, 2, 8, s), right_ops)


def solution(mesh):
    placed = (
        P("lsec", "rsec", None, None),
        P("op", "lsec", None, None),
        P("op", "rsec", None, None),
        P("op"),
    )
    return jax.shard_map(
        shards, mesh=mesh, in_specs=placed, out_specs=P("lsec", "rsec", "op", None), check_vma=False
    )
```

time: 179 us -> 42.7 us (0.24)
  the two profiles are of different devices: /device:TPU:1 before, /device:TPU:2 now
where the time goes in v1:
time: 42.7 us; the launch traced here: 42.6 us
  Pallas kernels  41.1 us (96%)
  local copies, waits for them, and re-layouts  1.47 us (3%)
    pallas_call x1, Pallas kernels, shards(): pl.pallas_call(kernel, out_shape=jax.ShapeDtypeStruct((nl, nr, s // (2 *...  41.1 us
    unnamed x1, local copies, waits for them, and re-layouts  1.47 us

profile of v1, /device:TPU:2, one launch (start us, length us, event | category | flops | bytes accessed | tf_op | source)
XLA Modules:
  0.0 42.6 jit_solution(13281550760944182842)
XLA Ops:
  0.0 41.1 %sigma.1 = f32[4,4,8,128]{3,2,1,0:T(8,128)} custom-call(s32[7]{0:T(128)} %shift.1, f32[4,4,128,128]{3,2,1,0:T(8,128)} %psi.1, f32[7,4,8,2,8,128]{5,4,3,2,1,0:T(8,128)} %bitcast.1, f32[7,4,128,128]{3,2,1,0:T(8,128)} %rop.1), custom_call_target="tpu_custom_call" | custom-call | tf_op jit(solution)/shard_map/sigma/pallas_call | solution.py:164
  41.1 1.5 %copy.6 = f32[4,4,8,128]{3,2,1,0:T(8,128)} copy(f32[4,4,8,128]{3,2,1,0:T(8,128)} %sigma.1) | data formatting | bytes 131072

commit v2 on v0

v2 whole, which is shorter than its diff:
```python
import jax
import jax.numpy as jnp
from jax import lax
from jax.experimental import pallas as pl
from jax.experimental.pallas import tpu as pltpu
from jax.sharding import PartitionSpec as P

MESH = pl.DeviceIdType.MESH
F32 = jnp.float32
BF16 = jnp.bfloat16
FAR = (4, 3, -3, 2, -2, 1, -1, 0)
GROUPS = ((0, 5), (5, 8))
NEAR = (0, 1, -1)
SLOT = {far: at for at, far in enumerate(FAR)}


def split(value):
    high = value.astype(BF16)
    return high, (value - high.astype(F32)).astype(BF16)


def kernel(
    shift, psi_hbm, lop_hbm, rop_hbm, out,
    psi, lop, rop, lcat, pcat, wcat, wlow, x, acc, peer, ring, final, load, send, recv,
):
    terms, nl, ny = lop.shape[0], lop.shape[1], lop.shape[2]
    nr, s = psi.shape[1], psi.shape[2]
    depth = terms * s

    op = lax.axis_index("op")
    lsec = lax.axis_index("lsec")
    rsec = lax.axis_index("rsec")
    n_lsec, n_rsec = lax.axis_size("lsec"), lax.axis_size("rsec")
    y, core = op // 2, op % 2

    def along(steps):
        return ((y + steps + ny) % ny) * 2 + core

    partner = {"op": y * 2 + (1 - core)}
    ring_to = {steps: {"op": along(steps)} for steps in (1, -1, 2, -2)}
    first_class = ((lsec > 0) & (lsec < n_lsec - 1)).astype(jnp.int32)
    classes = (first_class, 1 - first_class)

    def final_to(k, steps):
        sign = 1 - 2 * k
        return {
            "op": along(steps),
            "lsec": (lsec + sign + n_lsec) % n_lsec,
            "rsec": (rsec - sign + n_rsec) % n_rsec,
        }

    loads = []
    for l in range(nl):
        loads.append((psi_hbm.at[l], psi.at[l]))
        loads.append((lop_hbm.at[:, l], lop.at[:, l]))
    for r in range(nr):
        loads.append((rop_hbm.at[:, r], rop.at[:, r]))
    loads = [pltpu.make_async_copy(src, dst, load.at[i]) for i, (src, dst) in enumerate(loads)]
    for copy in loads:
        copy.start()

    barrier = pltpu.get_barrier_semaphore()
    greeted = [partner, *ring_to.values(), *(final_to(k, steps) for k in range(2) for steps in NEAR)]
    for who in greeted:
        pl.semaphore_signal(barrier, inc=1, device_id=who, device_id_type=MESH)

    sent = []

    def remote(src, dst, n, r, who):
        return pltpu.make_async_remote_copy(
            src_ref=src, dst_ref=dst, send_sem=send.at[r, n], recv_sem=recv.at[r, n], device_id=who, device_id_type=MESH
        )

    def start(copy):
        copy.start()
        sent.append(copy)

    def exchange(r, g):
        slots = pl.ds(GROUPS[g][0], GROUPS[g][1] - GROUPS[g][0])
        return remote(acc.at[r, 1 - core, slots], peer.at[r, slots], g, r, partner)

    def relays(r, stage):
        if stage == 0:
            return ((3, 1, 2), (-3, -1, -2), (4, 2, 2) if r % 2 == 0 else (4, -2, -2))
        return ((2, 1, 1), (-2, -1, -1))

    def relay_copy(r, k, stage, at):
        far, steps, _ = relays(r, stage)[at]
        n = 3 * stage + at
        return remote(acc.at[r, core, SLOT[far], k], ring.at[r, k, n], 2 + k * 5 + n, r, ring_to[steps])

    def start_relays(r, k, stage):
        for at in range(3 - stage):
            start(relay_copy(r, k, stage, at))

    def final_copy(r, k, at):
        far = NEAR[at]
        return remote(acc.at[r, core, SLOT[far], k], final.at[k, at, r], 12 + k * 3 + at, r, final_to(k, far))

    def split_left(g, l):
        first, last = GROUPS[g]
        for t in range(terms):
            for at in range(first, last):
                high, low = split(lop[t, l, (y + FAR[at] + ny) % ny])
                rows = pl.ds((t * (last - first) + at - first) * 16, 16)
                lcat[l, rows, 0:s] = high
                lcat[l, rows, s : 2 * s] = low

    def split_wave(l):
        for r in range(nr):
            high, low = split(psi[l, r])
            for k in range(2):
                pcat[l, r, k * s : (k + 1) * s, 0:s] = high
                pcat[l, r, k * s : (k + 1) * s, s : 2 * s] = low

    def split_right(r):
        for t in range(terms):
            weight = shift[t].astype(F32)
            for k, w in enumerate((weight, 1.0 - weight)):
                high, low = split(rop[t, r] * w)
                rows = pl.ds(k * s, s)
                wcat[r, rows, t * s : (t + 1) * s] = high
                wcat[r, rows, depth + t * s : depth + (t + 1) * s] = high
                wlow[r, rows, t * s : (t + 1) * s] = low

    def first_product(g, l, r):
        first, last = GROUPS[g]
        size = (last - first) * 16
        both = jnp.dot(lcat[l, 0 : terms * size], pcat[l, r], preferred_element_type=F32)
        high, low = split(both[:, 0:s] + both[:, s : 2 * s])
        rows = pl.ds(l * size, size)
        for t in range(terms):
            x[r, rows, t * s : (t + 1) * s] = high[t * size : (t + 1) * size]
            x[r, rows, depth + t * s : depth + (t + 1) * s] = low[t * size : (t + 1) * size]

    def second_product(g, r):
        first, last = GROUPS[g]
        size = (last - first) * 16
        nt = (((1,), (1,)), ((), ()))
        total = lax.dot_general(x[r, 0 : nl * size], wcat[r], nt, preferred_element_type=F32)
        total += lax.dot_general(x[r, 0 : nl * size, 0:depth], wlow[r], nt, preferred_element_type=F32)
        total = total.reshape(nl, last - first, 2, 8, 2 * s)
        for l in range(nl):
            for c in range(2):
                for k in range(2):
                    acc[r, c, first:last, k, l] = total[l, :, c, :, k * s : (k + 1) * s]

    def take_exchange(g, r):
        first, last = GROUPS[g]
        exchange(r, g).wait_recv()
        acc[r, core, first:last] += peer[r, first:last]

    def take_relays(r, k, stage):
        for at in range(3 - stage):
            relay_copy(r, k, stage, at).wait_recv()
        for at in range(3 - stage):
            far = relays(r, stage)[at][2]
            acc[r, core, SLOT[far], k] += ring[r, k, 3 * stage + at]

    for l in range(nl):
        loads[2 * l].wait()
        loads[2 * l + 1].wait()
        split_wave(l)
        split_left(0, l)
        for r in range(nr):
            first_product(0, l, r)
    for r in range(nr):
        loads[2 * nl + r].wait()
        split_right(r)
        second_product(0, r)
        if r == 0:
            pl.semaphore_wait(barrier, len(greeted))
        start(exchange(r, 0))
    for r in range(nr):
        take_exchange(0, r)
        start_relays(r, classes[0], 0)
    for r in range(nr):
        start_relays(r, classes[1], 0)
    for l in range(nl):
        split_left(1, l)
        for r in range(nr):
            first_product(1, l, r)
    for r in range(nr):
        second_product(1, r)
        start(exchange(r, 1))
    for k in classes:
        for r in range(nr):
            take_relays(r, k, 0)
            start_relays(r, k, 1)
    for r in range(nr):
        take_exchange(1, r)
        start(final_copy(r, classes[0], 0))
    for k in classes:
        for r in range(nr):
            take_relays(r, k, 1)
            for at in range(1, 3):
                start(final_copy(r, k, at))
        if k is classes[0]:
            for r in range(nr):
                start(final_copy(r, classes[1], 0))

    up_l = (lsec == 0).astype(jnp.int32)
    up_r = (rsec == n_rsec - 1).astype(jnp.int32)
    down_l = (lsec == n_lsec - 1).astype(jnp.int32)
    down_r = (rsec == 0).astype(jnp.int32)

    def picked(k, l, r):
        inside = (l >= 0) & (l < nl) & (r >= 0) & (r < nr)
        l, r = jnp.clip(l, 0, nl - 1), jnp.clip(r, 0, nr - 1)
        tile = sum(final[k, at, r, l] for at in range(1, len(NEAR))) + final[k, 0, r, l]
        return jnp.where(inside, tile, 0.0)

    for r in range(nr):
        for at in range(len(NEAR)):
            for k in range(2):
                final_copy(r, k, at).wait_recv()
    for l in range(nl):
        for r in range(nr):
            out[l, r] = picked(0, l - up_l, r + up_r) + picked(1, l + down_l, r - down_r)
    for copy in sent:
        copy.wait_send()


def shards(wavefn, left_ops, right_ops, term_shift):
    nl, nr, s = wavefn.shape[:3]
    terms = left_ops.shape[0]
    ny = lax.axis_size("op") // 2
    most = max(last - first for first, last in GROUPS) * 16
    hbm = pl.BlockSpec(memory_space=pl.ANY)
    left_ops = left_ops.reshape(terms, nl, ny, 16, s)
    return pl.pallas_call(
        kernel,
        out_shape=jax.ShapeDtypeStruct((nl, nr, 8, s), F32),
        in_specs=[pl.BlockSpec(memory_space=pltpu.SMEM), hbm, hbm, hbm],
        out_specs=pl.BlockSpec(memory_space=pltpu.VMEM),
        scratch_shapes=[
            pltpu.VMEM(wavefn.shape, F32),
            pltpu.VMEM(left_ops.shape, F32),
            pltpu.VMEM(right_ops.shape, F32),
            pltpu.VMEM((nl, terms * most, 2 * s), BF16),
            pltpu.VMEM((nl, nr, 2 * s, 2 * s), BF16),
            pltpu.VMEM((nr, 2 * s, 2 * terms * s), BF16),
            pltpu.VMEM((nr, 2 * s, terms * s), BF16),
            pltpu.VMEM((nr, nl * most, 2 * terms * s), BF16),
            pltpu.VMEM((nr, 2, ny, 2, nl, 8, s), F32),
            pltpu.VMEM((nr, ny, 2, nl, 8, s), F32),
            pltpu.VMEM((nr, 2, 5, nl, 8, s), F32),
            pltpu.VMEM((2, len(NEAR), nr, nl, 8, s), F32),
            pltpu.SemaphoreType.DMA((2 * nl + nr,)),
            pltpu.SemaphoreType.DMA((nr, 18)),
            pltpu.SemaphoreType.DMA((nr, 18)),
        ],
        compiler_params=pltpu.CompilerParams(collective_id=0, has_side_effects=True, vmem_limit_bytes=60 * 2**20),
        name="sigma",
    )(term_shift, wavefn, left_ops, right_ops)


def solution(mesh):
    placed = (
        P("lsec", "rsec", None, None),
        P("op", "lsec", None, None),
        P("op", "rsec", None, None),
        P("op"),
    )
    return jax.shard_map(
        shards, mesh=mesh, in_specs=placed, out_specs=P("lsec", "rsec", "op", None), check_vma=False
    )
```

time: 179 us -> 37.8 us (0.21)
  waiting for transfers between devices: 98.3 us -> 0 us
  Pallas kernels: 0 us -> 36.1 us
  matrix products: 35.1 us -> 0 us
  starting transfers between devices: 21.1 us -> 0 us
  between operations: 13.6 us -> 0.01 us
  other arithmetic: 4.04 us -> 0 us
  local copies, waits for them, and re-layouts: 5.08 us -> 1.47 us
    reduce_scatter x1 -> x0, waiting for transfers between devices: 58.2 us -> none  [shards(): return lax.psum_scatter(moved, 'op', scatter_dimension=2, tiled=True)]
    ppermute x4 -> x0, waiting for transfers between devices: 40.1 us -> none  [from_behind(): lax.ppermute(value, axis, [(i, (i + by) % count) for i in range(count)])]
    pallas_call x0 -> x1, Pallas kernels: none -> 36.1 us  [shards(): pl.pallas_call(kernel, out_shape=jax.ShapeDtypeStruct((nl, nr, 8, s), F32...]
    dot_general x3 -> x0, matrix products: 35.1 us -> none  [the longest x1 13.3 us: shards(): jnp.einsum('tlrik,trmk->lrim', inner * (1.0 - weight), right_ops, precisi...]
    ppermute x4 -> x0, starting transfers between devices: 21.1 us -> none  [from_behind(): lax.ppermute(value, axis, [(i, (i + by) % count) for i in range(count)])]
    dynamic_slice x2 -> x0, local copies, waits for them, and re-layouts: 3.54 us -> none  [roll_slots(): return lax.dynamic_slice_in_dim(padded, 1 - carry, count, dim)]
    add x1 -> x0, other arithmetic: 2.59 us -> none  [shards(): right_move(left_move(rising, 1), -1) + right_move(left_move(falling, -1), 1)]
  transfers between devices with their start and end apart: 5 -> 0, of which waited for: 5 -> 0; matrix products, arithmetic and copies ran while one was open for 9% -> 0% of each run, Pallas kernels for 0% -> 0%
where the time goes in v2:
time: 37.8 us; the launch traced here: 37.6 us
  Pallas kernels  36.1 us (96%)
  local copies, waits for them, and re-layouts  1.47 us (4%)
    pallas_call x1, Pallas kernels, shards(): pl.pallas_call(kernel, out_shape=jax.ShapeDtypeStruct((nl, nr, 8, s), F32...  36.1 us
    unnamed x1, local copies, waits for them, and re-layouts  1.47 us

profile of v2, /device:TPU:1, one launch (start us, length us, event | category | flops | bytes accessed | tf_op | source)
XLA Modules:
  0.0 37.6 jit_solution(13511543586776833265)
XLA Ops:
  0.0 36.1 %sigma.1 = f32[4,4,8,128]{3,2,1,0:T(8,128)} custom-call(s32[7]{0:T(128)} %shift.1, f32[4,4,128,128]{3,2,1,0:T(8,128)} %psi_hbm.1, f32[7,4,8,16,128]{4,3,2,1,0:T(8,128)} %bitcast.1, f32[7,4,128,128]{3,2,1,0:T(8,128)} %rop_hbm.1), custom_call_target="tpu_custom_call" | custom-call | tf_op jit(solution)/shard_map/sigma/pallas_call | solution.py:231
  36.1 1.5 %copy.6 = f32[4,4,8,128]{3,2,1,0:T(8,128)} copy(f32[4,4,8,128]{3,2,1,0:T(8,128)} %sigma.1) | data formatting | bytes 131072

commit v3 on v2

--- a/solution.py
+++ b/solution.py
@@ -230,7 +230,7 @@
     left_ops = left_ops.reshape(terms, nl, ny, 16, s)
     return pl.pallas_call(
         kernel,
-        out_shape=jax.ShapeDtypeStruct((nl, nr, 8, s), F32),
+        out_shape=pltpu.VMEM((nl, nr, 8, s), F32),
         in_specs=[pl.BlockSpec(memory_space=pltpu.SMEM), hbm, hbm, hbm],
         out_specs=pl.BlockSpec(memory_space=pltpu.VMEM),
         scratch_shapes=[

time: 37.8 us -> 36.3 us (0.960)
  local copies, waits for them, and re-layouts: 1.47 us -> 0.63 us
  Pallas kernels: 36.1 us -> 35.5 us
    unnamed x1, local copies, waits for them, and re-layouts: 1.47 us -> 0.63 us
    pallas_call x1, Pallas kernels: 36.1 us -> 35.5 us  [shards(): pl.pallas_call(kernel, out_shape=pltpu.VMEM((nl, nr, 8, s), F32), in_spec...]
where the time goes in v3:
time: 36.3 us; the launch traced here: 36.1 us
  Pallas kernels  35.5 us (98%)
  local copies, waits for them, and re-layouts  0.63 us (2%)
    pallas_call x1, Pallas kernels, shards(): pl.pallas_call(kernel, out_shape=pltpu.VMEM((nl, nr, 8, s), F32), in_spec...  35.5 us

profile of v3, /device:TPU:1, one launch (start us, length us, event | category | flops | bytes accessed | tf_op | source)
XLA Modules:
  0.0 36.1 jit_solution(9306245972924577272)
XLA Ops:
  0.0 35.5 %sigma.1 = f32[4,4,8,128]{3,2,1,0:T(8,128)S(1)} custom-call(s32[7]{0:T(128)} %shift.1, f32[4,4,128,128]{3,2,1,0:T(8,128)} %psi_hbm.1, f32[7,4,8,16,128]{4,3,2,1,0:T(8,128)} %bitcast.1, f32[7,4,128,128]{3,2,1,0:T(8,128)} %rop_hbm.1), custom_call_target="tpu_custom_call" | custom-call | tf_op jit(solution)/shard_map/sigma/pallas_call | solution.py:231
  35.5 0.6 %copy.6 = f32[4,4,8,128]{3,2,1,0:T(8,128)} copy(f32[4,4,8,128]{3,2,1,0:T(8,128)S(1)} %sigma.1) | data formatting | bytes 131072

commit v4 on v3

--- a/solution.py
+++ b/solution.py
@@ -9,7 +9,7 @@
 F32 = jnp.float32
 BF16 = jnp.bfloat16
 FAR = (4, 3, -3, 2, -2, 1, -1, 0)
-GROUPS = ((0, 5), (5, 8))
+GROUPS = ((0, 3), (3, 8))
 NEAR = (0, 1, -1)
 SLOT = {far: at for at, far in enumerate(FAR)}
 
@@ -183,12 +183,14 @@
     for r in range(nr):
         second_product(1, r)
         start(exchange(r, 1))
-    for k in classes:
-        for r in range(nr):
-            take_relays(r, k, 0)
-            start_relays(r, k, 1)
     for r in range(nr):
         take_exchange(1, r)
+        take_relays(r, classes[0], 0)
+        start_relays(r, classes[0], 1)
+    for r in range(nr):
+        take_relays(r, classes[1], 0)
+        start_relays(r, classes[1], 1)
+    for r in range(nr):
         start(final_copy(r, classes[0], 0))
     for k in classes:
         for r in range(nr):

time: 36.3 us -> 36 us (level)
  no operation moved by 1% of the time
where the time goes in v4:
time: 36 us; the launch traced here: 35.9 us
  Pallas kernels  35.2 us (98%)
  local copies, waits for them, and re-layouts  0.63 us (2%)
    pallas_call x1, Pallas kernels, shards(): pl.pallas_call(kernel, out_shape=pltpu.VMEM((nl, nr, 8, s), F32), in_spec...  35.2 us

profile of v4, /device:TPU:1, one launch (start us, length us, event | category | flops | bytes accessed | tf_op | source)
XLA Modules:
  0.0 35.9 jit_solution(1197725195036454547)
XLA Ops:
  0.0 35.2 %sigma.1 = f32[4,4,8,128]{3,2,1,0:T(8,128)S(1)} custom-call(s32[7]{0:T(128)} %shift.1, f32[4,4,128,128]{3,2,1,0:T(8,128)} %psi_hbm.1, f32[7,4,8,16,128]{4,3,2,1,0:T(8,128)} %bitcast.1, f32[7,4,128,128]{3,2,1,0:T(8,128)} %rop_hbm.1), custom_call_target="tpu_custom_call" | custom-call | tf_op jit(solution)/shard_map/sigma/pallas_call | solution.py:233
  35.2 0.6 %copy.6 = f32[4,4,8,128]{3,2,1,0:T(8,128)} copy(f32[4,4,8,128]{3,2,1,0:T(8,128)S(1)} %sigma.1) | data formatting | bytes 131072
